TPU v7x, 32 devices: a whole 2x2x4 slice. The times are simulated.
32 devices in a mesh: group: 2 (over x), expert: 16 (over z, y, core).
Axes of the slice: x: 2, y: 2, z: 4, core: 2. Of those that a mesh axis runs over, the one named last changes fastest.
Arguments:
- tokens: bfloat16 [128, 7168], P(('group', 'expert')), parts along dimension 0, may hold values from -6 to 6
- expert_ids: int32 [128, 2], P(('group', 'expert')), parts along dimension 0, may hold values from 0 to 1, all different within a row; in each aligned block of 4 rows (0 to 3, 4 to 7, ...) at most 4 rows name the same one
- gate_codes: int32 [128, 2], P(('group', 'expert')), parts along dimension 0, may hold values from 1 to 65535
- gate_weight: bfloat16 [16, 7168, 256], P('expert'), may hold values from -0.0625 to 0.0625
- up_weight: bfloat16 [16, 7168, 256], P('expert'), may hold values from -0.0625 to 0.0625
- down_weight: bfloat16 [16, 256, 7168], P('expert'), may hold values from -0.125 to 0.125
- target_basis: bfloat16 [7168, 512], P('expert'), may hold values from -0.0625 to 0.0625
Outputs:
- targets: bfloat16 [128, 512], P(('group', 'expert')), parts along dimension 0
There are 2 independent parts, one for each index of `group`. A program takes and returns all parts, laid end to end along the dimension named above; an argument that names none is the same for every part. Nothing has to cross between parts.
Inputs may be any that keep to these rules, and one draw needn't show every extreme that they name: `expert_ids`: each row names 2 different experts; among the 4 rows of one device no expert is named more than 4 times, a bound that some block reaches.
All inputs are finite; a program needn't handle non-finite values.
Results may differ from a plain program's by a relative error of at most 0.0057.
Values may be sent and summed in bfloat16 or wider, within the bound.
No kernel may reach another device: no remote copies, remote signals or barrier semaphores. Data moves between devices by JAX's collectives and lax.ppermute only.
A program may use at most 128 MiB of HBM per device.

v0:
```python
import jax
import jax.numpy as jnp
from jax import lax
from jax.sharding import PartitionSpec as P

SLICES = 8


def run_expert(received, gate_weight, up_weight, down_weight):
    sources, slots, feature_width = received.shape
    row_block = received.reshape(sources * slots, feature_width)
    gate_act = jnp.dot(row_block, gate_weight[0], preferred_element_type=jnp.float32)
    up_act = jnp.dot(row_block, up_weight[0], preferred_element_type=jnp.float32)
    hidden = (jax.nn.silu(gate_act) * up_act).astype(jnp.bfloat16)
    expert_part = jnp.dot(hidden, down_weight[0], preferred_element_type=jnp.float32).astype(
        jnp.bfloat16
    )
    return expert_part.reshape(sources, slots, feature_width)


def shards(tokens, expert_ids, gate_codes, gate_weight, up_weight, down_weight, target_basis):
    token_count, feature_width = tokens.shape
    pick_count = expert_ids.shape[1]
    owner_count = lax.axis_size("expert")
    expert_count = owner_count // SLICES
    capacity = min(token_count, max(2, 5 * token_count * pick_count // (4 * expert_count)))
    rank_width = target_basis.shape[1]
    flat_ids = expert_ids.reshape(-1)
    onehot = (flat_ids[:, None] == jnp.arange(expert_count, dtype=jnp.int32)[None, :]).astype(
        jnp.int32
    )
    before = jnp.cumsum(onehot, axis=0) - onehot
    slot_rank = jnp.sum(before * onehot, axis=1)
    slot_index = flat_ids * capacity + slot_rank
    row_token = jnp.arange(token_count * pick_count, dtype=jnp.int32) // pick_count
    slot_table = (
        jnp.full((expert_count * capacity,), token_count, jnp.int32).at[slot_index].set(row_token)
    )
    padded = jnp.concatenate([tokens, jnp.zeros((1, feature_width), tokens.dtype)], axis=0)
    per_expert_rows = padded[slot_table].reshape(expert_count, 1, capacity, feature_width)
    outgoing = jnp.broadcast_to(per_expert_rows, (expert_count, SLICES, capacity, feature_width))
    outgoing = outgoing.reshape(owner_count, capacity, feature_width)
    full_basis = lax.all_gather(target_basis, "expert", axis=0, tiled=True)
    expert_part = run_expert(
        lax.all_to_all(outgoing, "expert", split_axis=0, concat_axis=0, tiled=True),
        gate_weight,
        up_weight,
        down_weight,
    )
    result = jnp.einsum("skd,dr->skr", expert_part, full_basis, preferred_element_type=jnp.float32)
    returned = lax.all_to_all(result, "expert", split_axis=0, concat_axis=0, tiled=True)
    summed = jnp.sum(returned.reshape(expert_count, SLICES, capacity, rank_width), axis=1)
    projected = summed.reshape(expert_count * capacity, rank_width)[slot_index]
    codes_float = gate_codes.astype(jnp.float32)
    weights = 2.5 * codes_float / jnp.sum(codes_float, axis=1, keepdims=True)
    projected = projected.reshape(token_count, pick_count, rank_width)
    return jnp.sum(weights[:, :, None] * projected, axis=1).astype(jnp.bfloat16)


def solution(mesh):
    in_specs = (
        P(("group", "expert"), None),
        P(("group", "expert"), None),
        P(("group", "expert"), None),
        P("expert", None, None),
        P("expert", None, None),
        P("expert", None, None),
        P("expert", None),
    )
    out_specs = P(("group", "expert"), None)
    return jax.shard_map(shards, mesh=mesh, in_specs=in_specs, out_specs=out_specs, check_vma=False)
```

profile of v0, /device:TPU:0, one launch (start us, length us, event | category | flops | bytes accessed | tf_op | source)
XLA Modules:
  0.0 121.8 jit_solution(8186890199680378276)
XLA Ops:
  6.5 0.0 copy-start
  6.5 0.0 all-gather.2.cloned.1.call-start
  6.5 0.7 all-gather.2.cloned.1.call-update
  7.3 0.8 copy.25
  8.0 0.1 eq.15
  8.1 0.7 broadcast_multiply_fusion
  8.8 0.1 copy.24
  8.9 0.1 mul.37
  9.0 0.2 reduce_window_sum.11
  9.2 0.8 concatenate.3
  10.1 0.6 scatter_custom_fusion
  10.7 0.6 gather_fusion
  11.3 0.1 broadcast_in_dim.7
  11.4 1.2 broadcast_in_dim.8
  12.5 7.4 %all-to-all-start = ((bf16[16,4,7168]{2,1,0:T(4,128)(2,1)}), bf16[16,4,7168]{2,1,0:T(4,128)(2,1)S(1)}, u32[]{:S(2)}, u32[]{:S(2)}) async-start(bf16[16,4,7168]{2,1,0:T(4,128)(2,1)} %bitcast.2), calls=%async_computation | async-start | bytes 1835008 | tf_op jit(solution)/shard_map/all_to_all | solution.py:45
  19.9 0.0 copy-done
  20.0 35.1 %all-to-all-done = bf16[16,4,7168]{2,1,0:T(4,128)(2,1)S(1)} async-done(((bf16[16,4,7168]{2,1,0:T(4,128)(2,1)}), bf16[16,4,7168]{2,1,0:T(4,128)(2,1)S(1)}, u32[]{:S(2)}, u32[]{:S(2)}) %all-to-all-start) | async-done | bytes 917536 | tf_op jit(solution)/shard_map/all_to_all | solution.py:45
  55.1 0.2 reshape.53
  55.3 2.8 %fusion.5 = f32[64,256]{1,0:T(8,128)S(1)} fusion(bf16[64,7168]{1,0:T(8,128)(2,1)S(1)} %reshape.53, bf16[1,7168,256]{2,1,0:T(8,128)(2,1)} %param.10), kind=kOutput, calls=%fused_computation.9 | convolution fusion | flops 234881024 | bytes 4653056 | tf_op jit(solution)/shard_map/dot_general | solution.py:12
  58.0 5.5 %convolution_convert_fusion = bf16[64,7168]{1,0:T(8,128)(2,1)S(1)} fusion(bf16[1,256,7168]{2,1,0:T(8,128)(2,1)} %param.12, bf16[64,7168]{1,0:T(8,128)(2,1)S(1)} %reshape.53, bf16[1,7168,256]{2,1,0:T(8,128)(2,1)} %param.11, f32[64,256]{1,0:T(8,128)S(1)} %fusion.5), kind=kOutput, calls=%fused_computation.3 | convolution fusion | flops 470319104 | bytes 9240576 | tf_op jit(solution)/shard_map/dot_general | solution.py:15
  63.5 0.3 reshape.54
  63.8 33.4 %all-gather.2.cloned.1.call-done = bf16[7168,512]{1,0:T(8,128)(2,1)} async-done(((bf16[448,512]{1,0:T(8,128)(2,1)}), bf16[7168,512]{1,0:T(8,128)(2,1)}) %all-gather.2.cloned.1.call-update) | async-done | bytes 7340048 | tf_op jit(solution)/shard_map/all_gather | solution.py:43
  97.3 4.2 %fusion = f32[16,4,512]{2,0,1:T(8,128)S(1)} fusion(bf16[7168,512]{1,0:T(8,128)(2,1)} %all-gather.2.cloned.1.call-done, bf16[16,4,7168]{2,1,0:T(4,128)(2,1)S(1)} %reshape.54), kind=kOutput, calls=%fused_computation.4 | convolution fusion | flops 469762048 | bytes 8388608 | tf_op jit(solution)/shard_map/skd,dr->skr/dot_general | solution.py:50
  101.5 0.7 copy.27
  102.2 3.5 %all-to-all-start.1 = ((f32[16,4,512]{2,1,0:T(4,128)}), f32[16,4,512]{2,1,0:T(4,128)S(1)}, u32[]{:S(2)}, u32[]{:S(2)}) async-start(f32[16,4,512]{2,1,0:T(4,128)} %copy.27), calls=%async_computation.1 | async-start | bytes 262144 | tf_op jit(solution)/shard_map/all_to_all | solution.py:51
  105.8 0.1 copy.23
  105.9 7.8 %all-to-all-done.1 = f32[16,4,512]{2,1,0:T(4,128)S(1)} async-done(((f32[16,4,512]{2,1,0:T(4,128)}), f32[16,4,512]{2,1,0:T(4,128)S(1)}, u32[]{:S(2)}, u32[]{:S(2)}) %all-to-all-start.1) | async-done | bytes 131104 | tf_op jit(solution)/shard_map/all_to_all | solution.py:51
  113.7 0.6 gather_fusion.1
  114.2 0.7 multiply_reduce_fusion
  (12 shorter events, 0.1 us)
Async XLA Ops:
  6.5 13.4 %copy-start = (s32[4,2]{0,1:T(2,128)S(1)}, s32[4,2]{0,1:T(2,128)}, u32[]{:S(2)}) copy-start(s32[4,2]{0,1:T(2,128)} %param.9) | copy-start | bytes 100
  6.5 90.7 %all-gather.2.cloned.1.call-start = ((), (), s32[]{:S(2)}) async-start(), calls=%async_computation.2 | async-start | bytes 7798784 | tf_op jit(solution)/shard_map/all_gather | solution.py:43
  12.5 42.5 %all-to-all-start = ((bf16[16,4,7168]{2,1,0:T(4,128)(2,1)}), bf16[16,4,7168]{2,1,0:T(4,128)(2,1)S(1)}, u32[]{:S(2)}, u32[]{:S(2)}) async-start(bf16[16,4,7168]{2,1,0:T(4,128)(2,1)} %bitcast.2), calls=%async_computation | async-start | bytes 1835008 | tf_op jit(solution)/shard_map/all_to_all | solution.py:45
  102.2 11.4 %all-to-all-start.1 = ((f32[16,4,512]{2,1,0:T(4,128)}), f32[16,4,512]{2,1,0:T(4,128)S(1)}, u32[]{:S(2)}, u32[]{:S(2)}) async-start(f32[16,4,512]{2,1,0:T(4,128)} %copy.27), calls=%async_computation.1 | async-start | bytes 262144 | tf_op jit(solution)/shard_map/all_to_all | solution.py:51
Sparse Core Ops, SparseCore 0:
  9.6 87.5 all-gather.1
where the time goes:
time: 122 us
  waiting for transfers between devices  77 us (63%)
  between operations  13.5 us (11%)
  matrix products  12.4 us (10%)
  starting transfers between devices  10.9 us (9%)
  local copies, waits for them, and re-layouts  6.25 us (5%)
  other arithmetic  1.66 us (1%)
    all_to_all x1, waiting for transfers between devices, shards(): lax.all_to_all(outgoing, 'expert', split_axis=0, concat_axis=0, tiled=True)  35.1 us
    all_gather x1, waiting for transfers between devices, shards(): full_basis = lax.all_gather(target_basis, 'expert', axis=0, tiled=True)  33.4 us
    all_to_all x1, waiting for transfers between devices, shards(): lax.all_to_all(result, 'expert', split_axis=0, concat_axis=0, tiled=True)  7.76 us
    all_to_all x1, starting transfers between devices, shards(): lax.all_to_all(outgoing, 'expert', split_axis=0, concat_axis=0, tiled=True)  7.41 us
    dot_general x1, matrix products, run_expert(): jnp.dot(hidden, down_weight[0], preferred_element_type=jnp.float32)  5.45 us
    dot_general x1, matrix products, shards(): jnp.einsum('skd,dr->skr', expert_part, full_basis, preferred_element_type...  4.23 us
    all_to_all x1, starting transfers between devices, shards(): lax.all_to_all(result, 'expert', split_axis=0, concat_axis=0, tiled=True)  3.51 us
    dot_general x1, matrix products, run_expert(): jnp.dot(row_block, gate_weight[0], preferred_element_type=jnp.float32)  2.76 us
  transfers between devices with their start and end apart: 3, of which 3 were waited for; matrix products, arithmetic and copies ran while one was open for 12% of the time, Pallas kernels for 0%

commit v1 on v0

--- a/solution.py
+++ b/solution.py
@@ -40,14 +40,43 @@
     per_expert_rows = padded[slot_table].reshape(expert_count, 1, capacity, feature_width)
     outgoing = jnp.broadcast_to(per_expert_rows, (expert_count, SLICES, capacity, feature_width))
     outgoing = outgoing.reshape(owner_count, capacity, feature_width)
-    full_basis = lax.all_gather(target_basis, "expert", axis=0, tiled=True)
     expert_part = run_expert(
         lax.all_to_all(outgoing, "expert", split_axis=0, concat_axis=0, tiled=True),
         gate_weight,
         up_weight,
         down_weight,
     )
-    result = jnp.einsum("skd,dr->skr", expert_part, full_basis, preferred_element_type=jnp.float32)
+    size, index, span = (lax.axis_size("expert"), lax.axis_index("expert"), target_basis.shape[0])
+    upward = [(i, (i + 1) % size) for i in range(size)]
+    left = [(i, (i - 1) % size) for i in range(size)]
+    halfway = size // 2
+    from_left = from_right = target_basis
+    result = jnp.einsum(
+        "skd,dr->skr",
+        lax.dynamic_slice_in_dim(expert_part, index * span, target_basis.shape[0], axis=2),
+        target_basis,
+        preferred_element_type=jnp.float32,
+    )
+    for step in range(1, halfway + 1):
+        from_left = lax.ppermute(from_left, "expert", upward)
+        if step < size - halfway:
+            from_right = lax.ppermute(from_right, "expert", left)
+            result = result + jnp.einsum(
+                "skd,dr->skr",
+                lax.dynamic_slice_in_dim(
+                    expert_part, (index + step) % size * span, from_right.shape[0], axis=2
+                ),
+                from_right,
+                preferred_element_type=jnp.float32,
+            )
+        result = result + jnp.einsum(
+            "skd,dr->skr",
+            lax.dynamic_slice_in_dim(
+                expert_part, (index - step) % size * span, from_left.shape[0], axis=2
+            ),
+            from_left,
+            preferred_element_type=jnp.float32,
+        )
     returned = lax.all_to_all(result, "expert", split_axis=0, concat_axis=0, tiled=True)
     summed = jnp.sum(returned.reshape(expert_count, SLICES, capacity, rank_width), axis=1)
     projected = summed.reshape(expert_count * capacity, rank_width)[slot_index]

time: 122 us -> 144 us (1.18)
  starting transfers between devices: 10.9 us -> 50.7 us
  between operations: 13.5 us -> 0.35 us
  waiting for transfers between devices: 77 us -> 67.2 us
  matrix products: 12.4 us -> 16.4 us
    ppermute x0 -> x15, waiting for transfers between devices: none -> 59.4 us  [the longest x8 59.4 us: shards(): from_left = lax.ppermute(from_left, 'expert', upward)]
    all_to_all x1, waiting for transfers between devices: 35.1 us -> 0.01 us  [shards(): lax.all_to_all(outgoing, 'expert', split_axis=0, concat_axis=0, tiled=True)]
    all_gather x1 -> x0, waiting for transfers between devices: 33.4 us -> none  [shards(): full_basis = lax.all_gather(target_basis, 'expert', axis=0, tiled=True)]
    ppermute x0 -> x15, starting transfers between devices: none -> 31.7 us  [the longest x7 31.1 us: shards(): from_right = lax.ppermute(from_right, 'expert', left)]
    all_to_all x1, starting transfers between devices: 3.51 us -> 11.6 us  [shards(): lax.all_to_all(result, 'expert', split_axis=0, concat_axis=0, tiled=True)]
    dot_general x1 -> x16, matrix products: 4.23 us -> 8.21 us  [the longest x7 4.45 us: shards(): jnp.einsum('skd,dr->skr', lax.dynamic_slice_in_dim(expert_part, (index +...]
  transfers between devices with their start and end apart: 3 -> 17, of which waited for: 3 -> 9; matrix products, arithmetic and copies ran while one was open for 12% -> 13% of each run, Pallas kernels for 0% -> 0%
where the time goes in v1:
time: 144 us
  waiting for transfers between devices  67.2 us (47%)
  starting transfers between devices  50.7 us (35%)
  matrix products  16.4 us (11%)
  local copies, waits for them, and re-layouts  7.57 us (5%)
  other arithmetic  1.66 us (1%)
    ppermute x8, waiting for transfers between devices, shards(): from_left = lax.ppermute(from_left, 'expert', upward)  59.4 us
    ppermute x7, starting transfers between devices, shards(): from_right = lax.ppermute(from_right, 'expert', left)  31.1 us
    all_to_all x1, starting transfers between devices, shards(): lax.all_to_all(result, 'expert', split_axis=0, concat_axis=0, tiled=True)  11.6 us
    all_to_all x1, waiting for transfers between devices, shards(): lax.all_to_all(result, 'expert', split_axis=0, concat_axis=0, tiled=True)  7.79 us
    all_to_all x1, starting transfers between devices, shards(): lax.all_to_all(outgoing, 'expert', split_axis=0, concat_axis=0, tiled=True)  7.41 us
    dot_general x1, matrix products, run_expert(): jnp.dot(hidden, down_weight[0], preferred_element_type=jnp.float32)  5.45 us
    dot_general x7, matrix products, shards(): jnp.einsum('skd,dr->skr', lax.dynamic_slice_in_dim(expert_part, (index +...  4.45 us
    dot_general x8, matrix products, shards(): jnp.einsum('skd,dr->skr', lax.dynamic_slice_in_dim(expert_part, (index -...  3.57 us
  transfers between devices with their start and end apart: 17, of which 9 were waited for; matrix products, arithmetic and copies ran while one was open for 13% of the time, Pallas kernels for 0%

profile of v1, /device:TPU:0, one launch (start us, length us, event | category | flops | bytes accessed | tf_op | source)
XLA Modules:
  0.0 143.9 jit_solution(13761975763164862819)
XLA Ops:
  0.0 0.8 copy.70
  0.8 0.7 broadcast_multiply_fusion
  2.6 0.8 concatenate.3
  3.5 0.6 gather_fusion
  4.2 1.2 broadcast_in_dim.8
  5.3 7.4 %all-to-all-start = ((bf16[16,4,7168]{2,1,0:T(4,128)(2,1)}), bf16[16,4,7168]{2,1,0:T(4,128)(2,1)S(1)}, u32[]{:S(2)}, u32[]{:S(2)}) async-start(bf16[16,4,7168]{2,1,0:T(4,128)(2,1)} %bitcast.2), calls=%async_computation | async-start | bytes 1835008 | tf_op jit(solution)/shard_map/all_to_all | solution.py:44
  13.2 4.0 %collective-permute-start = (bf16[448,512]{1,0:T(8,128)(2,1)S(1)}, bf16[448,512]{1,0:T(8,128)(2,1)}, u32[]{:S(2)}, u32[]{:S(2)}) collective-permute-start(bf16[448,512]{1,0:T(8,128)(2,1)S(1)} %copy-done), channel_id=1, source_target_pairs={{0,15},{1,0},{2,1},{3,2},{4,3},{5,4},{6,5},{7,6},{8,7},{9,8},{10,9... | collective-permute-start | bytes 1376264 | tf_op jit(solution)/shard_map/ppermute | solution.py:63
  17.2 21.3 %collective-permute-done.1 = bf16[448,512]{1,0:T(8,128)(2,1)S(1)} collective-permute-done((bf16[448,512]{1,0:T(8,128)(2,1)S(1)}, bf16[448,512]{1,0:T(8,128)(2,1)S(1)}, u32[]{:S(2)}, u32[]{:S(2)}) %collective-permute-start.1) | collective-permute-done | bytes 458784 | tf_op jit(solution)/shard_map/ppermute | solution.py:61
  38.5 4.4 %collective-permute-start.2 = (bf16[448,512]{1,0:T(8,128)(2,1)}, bf16[448,512]{1,0:T(8,128)(2,1)S(1)}, u32[]{:S(2)}, u32[]{:S(2)}) collective-permute-start(bf16[448,512]{1,0:T(8,128)(2,1)} %collective-permute-done), channel_id=1, source_target_pairs={{0,15},{1,0},{2,1},{3,2},{4,3},{5,4},{6,5},{7,6},{8,7},{9,8},{10,9... | collective-permute-start | bytes 1376264 | tf_op jit(solution)/shard_map/ppermute | solution.py:63
  43.0 6.3 %collective-permute-done.3 = bf16[448,512]{1,0:T(8,128)(2,1)S(1)} collective-permute-done((bf16[448,512]{1,0:T(8,128)(2,1)S(1)}, bf16[448,512]{1,0:T(8,128)(2,1)S(1)}, u32[]{:S(2)}, u32[]{:S(2)}) %collective-permute-start.3) | collective-permute-done | bytes 458784 | tf_op jit(solution)/shard_map/ppermute | solution.py:61
  49.3 4.6 %collective-permute-start.4 = (bf16[448,512]{1,0:T(8,128)(2,1)S(1)}, bf16[448,512]{1,0:T(8,128)(2,1)}, u32[]{:S(2)}, u32[]{:S(2)}) collective-permute-start(bf16[448,512]{1,0:T(8,128)(2,1)S(1)} %collective-permute-done.2), channel_id=1, source_target_pairs={{0,15},{1,0},{2,1},{3,2},{4,3},{5,4},{6,5},{7,6},{8,7},{9,8},{10,9... | collective-permute-start | bytes 1376264 | tf_op jit(solution)/shard_map/ppermute | solution.py:63
  53.9 6.0 %collective-permute-done.5 = bf16[448,512]{1,0:T(8,128)(2,1)} collective-permute-done((bf16[448,512]{1,0:T(8,128)(2,1)S(1)}, bf16[448,512]{1,0:T(8,128)(2,1)}, u32[]{:S(2)}, u32[]{:S(2)}) %collective-permute-start.5) | collective-permute-done | bytes 458784 | tf_op jit(solution)/shard_map/ppermute | solution.py:61
  60.0 4.8 %collective-permute-start.6 = (bf16[448,512]{1,0:T(8,128)(2,1)}, bf16[448,512]{1,0:T(8,128)(2,1)}, u32[]{:S(2)}, u32[]{:S(2)}) collective-permute-start(bf16[448,512]{1,0:T(8,128)(2,1)} %collective-permute-done.4), channel_id=1, source_target_pairs={{0,15},{1,0},{2,1},{3,2},{4,3},{5,4},{6,5},{7,6},{8,7},{9,8},{10,9... | collective-permute-start | bytes 1376264 | tf_op jit(solution)/shard_map/ppermute | solution.py:63
  64.9 2.8 %fusion.3 = f32[64,256]{1,0:T(8,128)S(1)} fusion(bf16[64,7168]{1,0:T(8,128)(2,1)S(1)} %reshape.53, bf16[1,7168,256]{2,1,0:T(8,128)(2,1)} %param.10), kind=kOutput, calls=%fused_computation.7 | convolution fusion | flops 234881024 | bytes 4653056 | tf_op jit(solution)/shard_map/dot_general | solution.py:12
  67.7 5.5 %convolution_convert_fusion = bf16[64,7168]{1,0:T(8,128)(2,1)S(1)} fusion(bf16[1,256,7168]{2,1,0:T(8,128)(2,1)} %param.12, bf16[64,7168]{1,0:T(8,128)(2,1)S(1)} %reshape.53, bf16[1,7168,256]{2,1,0:T(8,128)(2,1)} %param.11, f32[64,256]{1,0:T(8,128)S(1)} %fusion.3), kind=kOutput, calls=%fused_computation.3 | convolution fusion | flops 470319104 | bytes 9240576 | tf_op jit(solution)/shard_map/dot_general | solution.py:15
  73.5 1.2 constant_dynamic-slice_fusion
  75.2 1.2 convolution_add_fusion.8
  76.8 1.2 fusion.32
  78.0 1.2 fusion.9
  79.4 4.4 %collective-permute-start.8 = (bf16[448,512]{1,0:T(8,128)(2,1)}, bf16[448,512]{1,0:T(8,128)(2,1)S(1)}, u32[]{:S(2)}, u32[]{:S(2)}) collective-permute-start(bf16[448,512]{1,0:T(8,128)(2,1)} %collective-permute-done.6), channel_id=1, source_target_pairs={{0,15},{1,0},{2,1},{3,2},{4,3},{5,4},{6,5},{7,6},{8,7},{9,8},{10,9... | collective-permute-start | bytes 1376264 | tf_op jit(solution)/shard_map/ppermute | solution.py:63
  83.8 1.2 fusion.29
  85.0 1.2 fusion.8
  86.2 4.0 %collective-permute-done.9 = bf16[448,512]{1,0:T(8,128)(2,1)S(1)} collective-permute-done((bf16[448,512]{1,0:T(8,128)(2,1)}, bf16[448,512]{1,0:T(8,128)(2,1)S(1)}, u32[]{:S(2)}, u32[]{:S(2)}) %collective-permute-start.9) | collective-permute-done | bytes 458784 | tf_op jit(solution)/shard_map/ppermute | solution.py:61
  90.2 4.4 %collective-permute-start.10 = (bf16[448,512]{1,0:T(8,128)(2,1)S(1)}, bf16[448,512]{1,0:T(8,128)(2,1)S(1)}, u32[]{:S(2)}, u32[]{:S(2)}) collective-permute-start(bf16[448,512]{1,0:T(8,128)(2,1)S(1)} %collective-permute-done.8), channel_id=1, source_target_pairs={{0,15},{1,0},{2,1},{3,2},{4,3},{5,4},{6,5},{7,6},{8,7},{9,8},{10,9... | collective-permute-start | bytes 1376264 | tf_op jit(solution)/shard_map/ppermute | solution.py:63
  95.1 5.8 %collective-permute-done.11 = bf16[448,512]{1,0:T(8,128)(2,1)S(1)} collective-permute-done((bf16[448,512]{1,0:T(8,128)(2,1)S(1)}, bf16[448,512]{1,0:T(8,128)(2,1)S(1)}, u32[]{:S(2)}, u32[]{:S(2)}) %collective-permute-start.11) | collective-permute-done | bytes 458784 | tf_op jit(solution)/shard_map/ppermute | solution.py:61
  101.0 4.4 %collective-permute-start.12 = (bf16[448,512]{1,0:T(8,128)(2,1)S(1)}, bf16[448,512]{1,0:T(8,128)(2,1)S(1)}, u32[]{:S(2)}, u32[]{:S(2)}) collective-permute-start(bf16[448,512]{1,0:T(8,128)(2,1)S(1)} %collective-permute-done.10), channel_id=1, source_target_pairs={{0,15},{1,0},{2,1},{3,2},{4,3},{5,4},{6,5},{7,6},{8,7},{9,8},{10,9... | collective-permute-start | bytes 1376264 | tf_op jit(solution)/shard_map/ppermute | solution.py:63
  105.8 5.7 %collective-permute-done.13 = bf16[448,512]{1,0:T(8,128)(2,1)S(1)} collective-permute-done((bf16[448,512]{1,0:T(8,128)(2,1)S(1)}, bf16[448,512]{1,0:T(8,128)(2,1)S(1)}, u32[]{:S(2)}, u32[]{:S(2)}) %collective-permute-start.13) | collective-permute-done | bytes 458784 | tf_op jit(solution)/shard_map/ppermute | solution.py:61
  112.0 10.2 %collective-permute-done.14 = bf16[448,512]{1,0:T(8,128)(2,1)S(1)} collective-permute-done((bf16[448,512]{1,0:T(8,128)(2,1)S(1)}, bf16[448,512]{1,0:T(8,128)(2,1)S(1)}, u32[]{:S(2)}, u32[]{:S(2)}) %collective-permute-start.14) | collective-permute-done | bytes 458784 | tf_op jit(solution)/shard_map/ppermute | solution.py:61
  122.3 0.7 copy.87
  123.1 11.6 %all-to-all-start.1 = ((f32[16,4,512]{2,1,0:T(4,128)}), f32[16,4,512]{2,1,0:T(4,128)S(1)}, u32[]{:S(2)}, u32[]{:S(2)}) async-start(f32[16,4,512]{2,1,0:T(4,128)} %copy.87), calls=%async_computation.1 | async-start | bytes 262144 | tf_op jit(solution)/shard_map/all_to_all | solution.py:80
  134.8 7.8 %all-to-all-done.1 = f32[16,4,512]{2,1,0:T(4,128)S(1)} async-done(((f32[16,4,512]{2,1,0:T(4,128)}), f32[16,4,512]{2,1,0:T(4,128)S(1)}, u32[]{:S(2)}, u32[]{:S(2)}) %all-to-all-start.1) | async-done | bytes 131104 | tf_op jit(solution)/shard_map/all_to_all | solution.py:80
  143.2 0.7 multiply_reduce_fusion
  (66 shorter events, 5.2 us)
Async XLA Ops:
  0.0 12.7 %copy-start = (bf16[448,512]{1,0:T(8,128)(2,1)S(1)}, bf16[448,512]{1,0:T(8,128)(2,1)}, u32[]{:S(2)}) copy-start(bf16[448,512]{1,0:T(8,128)(2,1)} %param.13) | copy-start | bytes 1376260
  0.0 53.9 %copy-start.7 = (s32[4,2]{0,1:T(2,128)S(1)}, s32[4,2]{0,1:T(2,128)}, u32[]{:S(2)}) copy-start(s32[4,2]{0,1:T(2,128)} %param.9) | copy-start | bytes 100
  5.3 59.4 %all-to-all-start = ((bf16[16,4,7168]{2,1,0:T(4,128)(2,1)}), bf16[16,4,7168]{2,1,0:T(4,128)(2,1)S(1)}, u32[]{:S(2)}, u32[]{:S(2)}) async-start(bf16[16,4,7168]{2,1,0:T(4,128)(2,1)} %bitcast.2), calls=%async_computation | async-start | bytes 1835008 | tf_op jit(solution)/shard_map/all_to_all | solution.py:44
  12.7 25.8 %collective-permute-start.1 = (bf16[448,512]{1,0:T(8,128)(2,1)S(1)}, bf16[448,512]{1,0:T(8,128)(2,1)S(1)}, u32[]{:S(2)}, u32[]{:S(2)}) collective-permute-start(bf16[448,512]{1,0:T(8,128)(2,1)S(1)} %copy-done), channel_id=1, source_target_pairs={{0,1},{1,2},{2,3},{3,4},{4,5},{5,6},{6,7},{7,8},{8,9},{9,10},{10,1... | collective-permute-start | bytes 1376264 | tf_op jit(solution)/shard_map/ppermute | solution.py:61
  13.2 25.3 %collective-permute-start = (bf16[448,512]{1,0:T(8,128)(2,1)S(1)}, bf16[448,512]{1,0:T(8,128)(2,1)}, u32[]{:S(2)}, u32[]{:S(2)}) collective-permute-start(bf16[448,512]{1,0:T(8,128)(2,1)S(1)} %copy-done), channel_id=1, source_target_pairs={{0,15},{1,0},{2,1},{3,2},{4,3},{5,4},{6,5},{7,6},{8,7},{9,8},{10,9... | collective-permute-start | bytes 1376264 | tf_op jit(solution)/shard_map/ppermute | solution.py:63
  38.5 26.4 %copy-start.5 = (bf16[448,512]{1,0:T(8,128)(2,1)}, bf16[448,512]{1,0:T(8,128)(2,1)S(1)}, u32[]{:S(2)}) copy-start(bf16[448,512]{1,0:T(8,128)(2,1)S(1)} %collective-permute-done.1) | copy-start | bytes 1376260
  38.5 10.7 %collective-permute-start.3 = (bf16[448,512]{1,0:T(8,128)(2,1)S(1)}, bf16[448,512]{1,0:T(8,128)(2,1)S(1)}, u32[]{:S(2)}, u32[]{:S(2)}) collective-permute-start(bf16[448,512]{1,0:T(8,128)(2,1)S(1)} %collective-permute-done.1), channel_id=1, source_target_pairs={{0,1},{1,2},{2,3},{3,4},{4,5},{5,6},{6,7},{7,8},{8,9},{9,10},{10,1... | collective-permute-start | bytes 1376264 | tf_op jit(solution)/shard_map/ppermute | solution.py:61
  38.5 10.8 %collective-permute-start.2 = (bf16[448,512]{1,0:T(8,128)(2,1)}, bf16[448,512]{1,0:T(8,128)(2,1)S(1)}, u32[]{:S(2)}, u32[]{:S(2)}) collective-permute-start(bf16[448,512]{1,0:T(8,128)(2,1)} %collective-permute-done), channel_id=1, source_target_pairs={{0,15},{1,0},{2,1},{3,2},{4,3},{5,4},{6,5},{7,6},{8,7},{9,8},{10,9... | collective-permute-start | bytes 1376264 | tf_op jit(solution)/shard_map/ppermute | solution.py:63
  49.2 15.5 %copy-start.3 = (bf16[448,512]{1,0:T(8,128)(2,1)}, bf16[448,512]{1,0:T(8,128)(2,1)S(1)}, u32[]{:S(2)}) copy-start(bf16[448,512]{1,0:T(8,128)(2,1)S(1)} %collective-permute-done.3) | copy-start | bytes 1376260
  49.2 10.7 %collective-permute-start.5 = (bf16[448,512]{1,0:T(8,128)(2,1)S(1)}, bf16[448,512]{1,0:T(8,128)(2,1)}, u32[]{:S(2)}, u32[]{:S(2)}) collective-permute-start(bf16[448,512]{1,0:T(8,128)(2,1)S(1)} %collective-permute-done.3), channel_id=1, source_target_pairs={{0,1},{1,2},{2,3},{3,4},{4,5},{5,6},{6,7},{7,8},{8,9},{9,10},{10,1... | collective-permute-start | bytes 1376264 | tf_op jit(solution)/shard_map/ppermute | solution.py:61
  49.3 15.4 %copy-start.1 = (bf16[448,512]{1,0:T(8,128)(2,1)}, bf16[448,512]{1,0:T(8,128)(2,1)S(1)}, u32[]{:S(2)}) copy-start(bf16[448,512]{1,0:T(8,128)(2,1)S(1)} %collective-permute-done.2) | copy-start | bytes 1376260
  49.3 10.7 %collective-permute-start.4 = (bf16[448,512]{1,0:T(8,128)(2,1)S(1)}, bf16[448,512]{1,0:T(8,128)(2,1)}, u32[]{:S(2)}, u32[]{:S(2)}) collective-permute-start(bf16[448,512]{1,0:T(8,128)(2,1)S(1)} %collective-permute-done.2), channel_id=1, source_target_pairs={{0,15},{1,0},{2,1},{3,2},{4,3},{5,4},{6,5},{7,6},{8,7},{9,8},{10,9... | collective-permute-start | bytes 1376264 | tf_op jit(solution)/shard_map/ppermute | solution.py:63
  59.9 19.3 %collective-permute-start.7 = (bf16[448,512]{1,0:T(8,128)(2,1)}, bf16[448,512]{1,0:T(8,128)(2,1)}, u32[]{:S(2)}, u32[]{:S(2)}) collective-permute-start(bf16[448,512]{1,0:T(8,128)(2,1)} %collective-permute-done.5), channel_id=1, source_target_pairs={{0,1},{1,2},{2,3},{3,4},{4,5},{5,6},{6,7},{7,8},{8,9},{9,10},{10,1... | collective-permute-start | bytes 1376264 | tf_op jit(solution)/shard_map/ppermute | solution.py:61
  60.0 19.4 %collective-permute-start.6 = (bf16[448,512]{1,0:T(8,128)(2,1)}, bf16[448,512]{1,0:T(8,128)(2,1)}, u32[]{:S(2)}, u32[]{:S(2)}) collective-permute-start(bf16[448,512]{1,0:T(8,128)(2,1)} %collective-permute-done.4), channel_id=1, source_target_pairs={{0,15},{1,0},{2,1},{3,2},{4,3},{5,4},{6,5},{7,6},{8,7},{9,8},{10,9... | collective-permute-start | bytes 1376264 | tf_op jit(solution)/shard_map/ppermute | solution.py:63
  73.2 1.8 %copy-start.4 = (bf16[448,512]{1,0:T(8,128)(2,1)S(1)}, bf16[448,512]{1,0:T(8,128)(2,1)}, u32[]{:S(2)}) copy-start(bf16[448,512]{1,0:T(8,128)(2,1)} %copy-done.3) | copy-start | bytes 1376260
  73.2 3.4 %copy-start.2 = (bf16[448,512]{1,0:T(8,128)(2,1)S(1)}, bf16[448,512]{1,0:T(8,128)(2,1)}, u32[]{:S(2)}) copy-start(bf16[448,512]{1,0:T(8,128)(2,1)} %copy-done.1) | copy-start | bytes 1376260
  73.5 2.9 %copy-start.6 = (bf16[448,512]{1,0:T(8,128)(2,1)S(1)}, bf16[448,512]{1,0:T(8,128)(2,1)}, u32[]{:S(2)}) copy-start(bf16[448,512]{1,0:T(8,128)(2,1)} %copy-done.5) | copy-start | bytes 1376260
  79.3 11.0 %collective-permute-start.9 = (bf16[448,512]{1,0:T(8,128)(2,1)}, bf16[448,512]{1,0:T(8,128)(2,1)S(1)}, u32[]{:S(2)}, u32[]{:S(2)}) collective-permute-start(bf16[448,512]{1,0:T(8,128)(2,1)} %collective-permute-done.7), channel_id=1, source_target_pairs={{0,1},{1,2},{2,3},{3,4},{4,5},{5,6},{6,7},{7,8},{8,9},{9,10},{10,1... | collective-permute-start | bytes 1376264 | tf_op jit(solution)/shard_map/ppermute | solution.py:61
  79.4 10.9 %collective-permute-start.8 = (bf16[448,512]{1,0:T(8,128)(2,1)}, bf16[448,512]{1,0:T(8,128)(2,1)S(1)}, u32[]{:S(2)}, u32[]{:S(2)}) collective-permute-start(bf16[448,512]{1,0:T(8,128)(2,1)} %collective-permute-done.6), channel_id=1, source_target_pairs={{0,15},{1,0},{2,1},{3,2},{4,3},{5,4},{6,5},{7,6},{8,7},{9,8},{10,9... | collective-permute-start | bytes 1376264 | tf_op jit(solution)/shard_map/ppermute | solution.py:63
  90.2 10.7 %collective-permute-start.11 = (bf16[448,512]{1,0:T(8,128)(2,1)S(1)}, bf16[448,512]{1,0:T(8,128)(2,1)S(1)}, u32[]{:S(2)}, u32[]{:S(2)}) collective-permute-start(bf16[448,512]{1,0:T(8,128)(2,1)S(1)} %collective-permute-done.9), channel_id=1, source_target_pairs={{0,1},{1,2},{2,3},{3,4},{4,5},{5,6},{6,7},{7,8},{8,9},{9,10},{10,1... | collective-permute-start | bytes 1376264 | tf_op jit(solution)/shard_map/ppermute | solution.py:61
  90.2 10.7 %collective-permute-start.10 = (bf16[448,512]{1,0:T(8,128)(2,1)S(1)}, bf16[448,512]{1,0:T(8,128)(2,1)S(1)}, u32[]{:S(2)}, u32[]{:S(2)}) collective-permute-start(bf16[448,512]{1,0:T(8,128)(2,1)S(1)} %collective-permute-done.8), channel_id=1, source_target_pairs={{0,15},{1,0},{2,1},{3,2},{4,3},{5,4},{6,5},{7,6},{8,7},{9,8},{10,9... | collective-permute-start | bytes 1376264 | tf_op jit(solution)/shard_map/ppermute | solution.py:63
  100.9 10.6 %collective-permute-start.13 = (bf16[448,512]{1,0:T(8,128)(2,1)S(1)}, bf16[448,512]{1,0:T(8,128)(2,1)S(1)}, u32[]{:S(2)}, u32[]{:S(2)}) collective-permute-start(bf16[448,512]{1,0:T(8,128)(2,1)S(1)} %collective-permute-done.11), channel_id=1, source_target_pairs={{0,1},{1,2},{2,3},{3,4},{4,5},{5,6},{6,7},{7,8},{8,9},{9,10},{10,1... | collective-permute-start | bytes 1376264 | tf_op jit(solution)/shard_map/ppermute | solution.py:61
  101.0 10.8 %collective-permute-start.12 = (bf16[448,512]{1,0:T(8,128)(2,1)S(1)}, bf16[448,512]{1,0:T(8,128)(2,1)S(1)}, u32[]{:S(2)}, u32[]{:S(2)}) collective-permute-start(bf16[448,512]{1,0:T(8,128)(2,1)S(1)} %collective-permute-done.10), channel_id=1, source_target_pairs={{0,15},{1,0},{2,1},{3,2},{4,3},{5,4},{6,5},{7,6},{8,7},{9,8},{10,9... | collective-permute-start | bytes 1376264 | tf_op jit(solution)/shard_map/ppermute | solution.py:63
  111.5 10.6 %collective-permute-start.14 = (bf16[448,512]{1,0:T(8,128)(2,1)S(1)}, bf16[448,512]{1,0:T(8,128)(2,1)S(1)}, u32[]{:S(2)}, u32[]{:S(2)}) collective-permute-start(bf16[448,512]{1,0:T(8,128)(2,1)S(1)} %collective-permute-done.13), channel_id=1, source_target_pairs={{0,1},{1,2},{2,3},{3,4},{4,5},{5,6},{6,7},{7,8},{8,9},{9,10},{10,1... | collective-permute-start | bytes 1376264 | tf_op jit(solution)/shard_map/ppermute | solution.py:61
  123.1 19.5 %all-to-all-start.1 = ((f32[16,4,512]{2,1,0:T(4,128)}), f32[16,4,512]{2,1,0:T(4,128)S(1)}, u32[]{:S(2)}, u32[]{:S(2)}) async-start(f32[16,4,512]{2,1,0:T(4,128)} %copy.87), calls=%async_computation.1 | async-start | bytes 262144 | tf_op jit(solution)/shard_map/all_to_all | solution.py:80
